TPU v7x, 32 devices: a whole 2x2x4 slice. The times are simulated.
32 devices in a mesh: row: 4 (over y, x), col: 8 (over z, core).
Axes of the slice: x: 2, y: 2, z: 4, core: 2. Of those that a mesh axis runs over, the one named last changes fastest.
Arguments:
- features: bfloat16 [32768, 128], P(('row', 'col')), may hold values from -6 to 6
- pair_index: int32 [2, 4096], P(None, ('row', 'col')), may hold values from -1 to 63, as said below
- bins: int32 [4096, 128, 128], P(('row', 'col')), may hold values from 0 to 8, as said below
- plate_weight: bfloat16 [1024, 128], replicated, may hold values from -0.1875 to 0.1875
- tower_weight: bfloat16 [1024, 128], replicated, may hold values from -0.1875 to 0.1875
- norm_gain: float32 [128], replicated, may hold values from 0.1 to 1.9
- update_in: bfloat16 [256, 128], replicated, may hold values from -0.375 to 0.375
- update_out: bfloat16 [128, 128], replicated, may hold values from -0.5 to 0.5
Outputs:
- updated: bfloat16 [32768, 128], P(('row', 'col'))
Inputs may be any that keep to these rules, and one draw needn't show every extreme that they name: `pair_index`: row 0 is a cluster of the meeting device's plate (below 64), row 1 a cluster of its tower (below 32). The 128 slots of one meeting device hold its live pairs first and then -1 in both rows. No cluster pair is live twice on one device. Some device has all 128 slots live. `bins`: 8 marks an atom pair that is no neighbour.
All inputs are finite; a program needn't handle non-finite values.
Results may differ from a plain program's by a relative error of at most 0.008.
Values may be sent and summed in bfloat16 or wider, within the bound.
A program may use at most 128 MiB of HBM per device.

v0:
```python
import jax
import jax.numpy as jnp
from jax import lax
from jax.sharding import PartitionSpec as P

D = 128
CLUSTER = 128
BINS = 8


def block_basis(pair_index, bins, turn, group):
    start = turn * group
    plate_idx = lax.dynamic_slice_in_dim(pair_index[0], start, group)
    tower_idx = lax.dynamic_slice_in_dim(pair_index[1], start, group)
    block = lax.dynamic_slice_in_dim(bins, start, group, 0)
    live = plate_idx >= 0
    levels = jnp.arange(BINS, dtype=jnp.int32)
    basis = (
        (block[:, :, None, :] == levels[None, None, :, None]) & live[:, None, None, None]
    ).astype(jnp.bfloat16)
    return (jnp.maximum(plate_idx, 0), jnp.maximum(tower_idx, 0), basis)


def plate_side(basis, tower, tower_at, plate_weight):
    count = basis.shape[0]
    near_plate = jnp.einsum(
        "gakb,gbd->gakd", basis, tower[tower_at], preferred_element_type=jnp.float32
    ).astype(jnp.bfloat16)
    message = jnp.dot(
        near_plate.reshape(count * CLUSTER, BINS * D),
        plate_weight,
        preferred_element_type=jnp.float32,
    )
    return message.reshape(count, CLUSTER, D)


def tower_side(basis, plate, plate_at, tower_weight):
    count = basis.shape[0]
    near_tower = jnp.einsum(
        "gakb,gad->gbkd", basis, plate[plate_at], preferred_element_type=jnp.float32
    ).astype(jnp.bfloat16)
    message = jnp.dot(
        near_tower.reshape(count * CLUSTER, BINS * D),
        tower_weight,
        preferred_element_type=jnp.float32,
    )
    return message.reshape(count, CLUSTER, D)


def return_tower(tower_acc, own_rows):
    flat = tower_acc.reshape(-1, D)
    summed = lax.psum(flat.astype(jnp.bfloat16), "row").astype(jnp.float32)
    return lax.dynamic_slice_in_dim(summed, lax.axis_index("row") * own_rows, own_rows, 0)


def return_plate(plate_acc, own_rows):
    flat = plate_acc.reshape(-1, D)
    summed = lax.psum(flat.astype(jnp.bfloat16), "col").astype(jnp.float32)
    return lax.dynamic_slice_in_dim(summed, lax.axis_index("col") * own_rows, own_rows, 0)


def shards(
    features, pair_index, bins, plate_weight, tower_weight, norm_gain, update_in, update_out
):
    own_rows = features.shape[0]
    plate = lax.all_gather(features, "col", axis=0, tiled=True).reshape(-1, CLUSTER, D)
    tower = lax.all_gather(features, "row", axis=0, tiled=True).reshape(-1, CLUSTER, D)
    group = 8
    slots = bins.shape[0]
    turns = slots // group
    plate_zero = jnp.zeros((plate.shape[0], CLUSTER, D), jnp.float32)
    tower_zero = jnp.zeros((tower.shape[0], CLUSTER, D), jnp.float32)

    def tower_step(turn, tower_acc):
        plate_at, tower_at, basis = block_basis(pair_index, bins, turn, group)
        return tower_acc.at[tower_at].add(tower_side(basis, plate, plate_at, tower_weight))

    def plate_step(turn, plate_acc):
        plate_at, tower_at, basis = block_basis(pair_index, bins, turn, group)
        return plate_acc.at[plate_at].add(plate_side(basis, tower, tower_at, plate_weight))

    tower_acc = lax.fori_loop(0, turns, tower_step, tower_zero)
    tower_back = return_tower(tower_acc, own_rows)
    plate_acc = lax.fori_loop(0, turns, plate_step, plate_zero)
    plate_back = return_plate(plate_acc, own_rows)
    incoming = plate_back + tower_back
    scale = lax.rsqrt(jnp.mean(incoming * incoming, axis=1, keepdims=True) + 1e-06)
    normed = (incoming * scale * norm_gain[None, :]).astype(jnp.bfloat16)
    joined = jnp.concatenate([features, normed], axis=1)
    hidden = jax.nn.silu(jnp.dot(joined, update_in, preferred_element_type=jnp.float32)).astype(
        jnp.bfloat16
    )
    result = features.astype(jnp.float32) + jnp.dot(
        hidden, update_out, preferred_element_type=jnp.float32
    )
    return result.astype(jnp.bfloat16)


def solution(mesh):
    placed = (
        P(("row", "col"), None),
        P(None, ("row", "col")),
        P(("row", "col"), None, None),
        P(),
        P(),
        P(),
        P(),
        P(),
    )
    return jax.shard_map(
        shards, mesh=mesh, in_specs=placed, out_specs=P(("row", "col"), None), check_vma=False
    )
```

profile of v0, /device:TPU:0, one launch (start us, length us, event | category | flops | bytes accessed | tf_op | source)
XLA Modules:
  0.0 342.0 jit_solution(12358343995069311886)
XLA Ops:
  8.1 30.4 %all-gather.3.cloned.1.call-done = bf16[4096,128]{1,0:T(8,128)(2,1)} async-done(((bf16[1024,128]{1,0:T(8,128)(2,1)}), bf16[4096,128]{1,0:T(8,128)(2,1)}) %all-gather.3.cloned.1.call-update) | async-done | bytes 1048592 | tf_op jit(solution)/shard_map/all_gather | solution.py:67
  38.4 2.5 broadcast_in_dim.38
  40.9 126.6 %while.26 = (s32[]{:T(128)}, f32[64,128,128]{2,1,0:T(8,128)}, s32[2,128]{1,0:T(2,128)S(1)}, s32[128,128,128]{2,1,0:T(8,128)}, bf16[32,128,128]{2,1,0:T(8,128)(2,...) while((s32[]{:T(128)}, f32[64,128,128]{2,1,0:T(8,128)}, ...), condition=%wide.region_2.0_spmd, body=%wide.region_0.0_spmd.sunk | while | flops 540148736 | bytes 8919471 | solution.py:84
  46.0 2.7 scatter_fusion
  53.9 2.7 scatter_fusion
  61.8 2.7 scatter_fusion
  69.6 2.8 scatter_fusion
  77.6 2.8 scatter_fusion
  85.5 2.8 scatter_fusion
  93.4 2.8 scatter_fusion
  101.3 2.8 scatter_fusion
  109.2 2.8 scatter_fusion
  117.2 2.8 scatter_fusion
  125.1 2.8 scatter_fusion
  133.0 2.8 scatter_fusion
  140.9 2.8 scatter_fusion
  148.9 2.8 scatter_fusion
  156.8 2.8 scatter_fusion
  164.7 2.8 scatter_fusion
  167.5 3.9 %convert_element_type.54 = bf16[64,128,128]{2,1,0:T(8,128)(2,1)} convert(f32[64,128,128]{2,1,0:T(8,128)} %get-tuple-element.223) | non-fusion elementwise | flops 1048576 | bytes 6291456 | tf_op jit(solution)/shard_map/convert_element_type | solution.py:58
  172.4 105.5 %while.27 = (s32[]{:T(128)}, f32[32,128,128]{2,1,0:T(8,128)S(1)}, s32[2,128]{1,0:T(2,128)S(1)}, bf16[64,128,128]{2,1,0:T(8,128)(2,1)}, s32[128,128,128]{2,1,0:T(...) while((s32[]{:T(128)}, f32[32,128,128]{2,1,0:T(8,128)S(1)}, ...), condition=%wide.region_6.0_spmd, body=%wide.region_4.0_spmd.sunk | while | flops 540148736 | bytes 8919471 | solution.py:82
  185.6 2.2 gather_fusion.1
  212.0 2.2 gather_fusion.1
  279.1 52.6 %all-reduce.5.cloned.1.call-done = bf16[4096,128]{1,0:T(8,128)(2,1)} async-done(((bf16[4096,128]{1,0:T(8,128)(2,1)}), bf16[4096,128]{1,0:T(8,128)(2,1)}) %all-reduce.5.cloned.1.call-update) | async-done | bytes 1048592 | tf_op jit(solution)/shard_map/psum | solution.py:52
  (300 shorter events, 189.3 us)
Async XLA Ops:
  6.5 327.7 %copy-start = (bf16[256,128]{1,0:T(8,128)(2,1)S(1)}, bf16[256,128]{1,0:T(8,128)(2,1)}, u32[]{:S(2)}) copy-start(bf16[256,128]{1,0:T(8,128)(2,1)} %param.18) | copy-start | bytes 196612
  6.5 31.9 %all-gather.3.cloned.1.call-start = ((), (), s32[]{:S(2)}) async-start(), calls=%async_computation | async-start | bytes 1310720 | tf_op jit(solution)/shard_map/all_gather | solution.py:67
  7.3 164.2 %all-gather.5.cloned.1.call-start = ((), (), s32[]{:S(2)}) async-start(), calls=%async_computation.2 | async-start | bytes 2359296 | tf_op jit(solution)/shard_map/all_gather | solution.py:66
  8.0 271.1 %all-reduce.3.cloned.1.call-start = ((), (), s32[]{:S(2)}) async-start(), calls=%async_computation.1 | async-start | bytes 4194304 | tf_op jit(solution)/shard_map/psum | solution.py:58
  38.4 2.5 copy-start.1
  38.4 2.5 copy-start.4
  171.4 0.9 copy-start.2
  171.4 160.2 %all-reduce.5.cloned.1.call-start = ((), (), s32[]{:S(2)}) async-start(), calls=%async_computation.3 | async-start | bytes 2097152 | tf_op jit(solution)/shard_map/psum | solution.py:52
  277.8 55.1 %copy-start.5 = (f32[128]{0:T(128)S(1)}, f32[128]{0:T(128)}, u32[]{:S(2)}) copy-start(f32[128]{0:T(128)} %param.17) | copy-start | bytes 1540
  277.9 56.4 %copy-start.3 = (bf16[1024,128]{1,0:T(8,128)(2,1)S(1)}, bf16[1024,128]{1,0:T(8,128)(2,1)}, u32[]{:S(2)}) copy-start(bf16[1024,128]{1,0:T(8,128)(2,1)} %param.12) | copy-start | bytes 786436
  277.9 56.3 %copy-start.6 = (bf16[128,128]{1,0:T(8,128)(2,1)S(1)}, bf16[128,128]{1,0:T(8,128)(2,1)}, u32[]{:S(2)}) copy-start(bf16[128,128]{1,0:T(8,128)(2,1)} %param.19) | copy-start | bytes 98308
Sparse Core Ops, SparseCore 0:
  9.2 29.2 all-gather.2
  40.0 29.1 all-gather.4
  171.6 65.1 all-reduce.2
  279.2 52.4 all-reduce.4
where the time goes:
time: 346 us; the launch traced here: 342 us
  local copies, waits for them, and re-layouts  102 us (29%)
  waiting for transfers between devices  84.4 us (24%)
  other arithmetic  73.5 us (21%)
  matrix products  67 us (19%)
  between operations  13.2 us (4%)
    psum x1, waiting for transfers between devices, return_tower(): summed = lax.psum(flat.astype(jnp.bfloat16), 'row').astype(jnp.float32)  52.6 us
    scatter-add x16, other arithmetic, plate_step(): plate_acc.at[plate_at].add(plate_side(basis, tower, tower_at, plate_weight))  44.2 us
    gather x16, local copies, waits for them, and re-layouts, tower_side(): plate[plate_at]  35.2 us
    dynamic_slice x32, local copies, waits for them, and re-layouts, block_basis(): block = lax.dynamic_slice_in_dim(bins, start, group, 0)  34.4 us
    all_gather x1, waiting for transfers between devices, shards(): lax.all_gather(features, 'row', axis=0, tiled=True).reshape(-1, CLUSTER, D)  30.4 us
    gather x16, local copies, waits for them, and re-layouts, plate_side(): tower[tower_at]  29.2 us
    dot_general x16, matrix products, plate_side(): jnp.einsum('gakb,gbd->gakd', basis, tower[tower_at], preferred_element_ty...  20.9 us
    dot_general x16, matrix products, tower_side(): jnp.einsum('gakb,gad->gbkd', basis, plate[plate_at], preferred_element_ty...  20.8 us
  transfers between devices with their start and end apart: 4, of which 2 were waited for; matrix products, arithmetic and copies ran while one was open for 70% of the time, Pallas kernels for 0%

commit v1 on v0

--- a/solution.py
+++ b/solution.py
@@ -49,7 +49,7 @@
 
 def return_tower(tower_acc, own_rows):
     flat = tower_acc.reshape(-1, D)
-    summed = lax.psum(flat.astype(jnp.bfloat16), "row").astype(jnp.float32)
+    summed = jnp.sum(lax.all_gather(flat.astype(jnp.bfloat16), "row"), axis=0).astype(jnp.float32)
     return lax.dynamic_slice_in_dim(summed, lax.axis_index("row") * own_rows, own_rows, 0)
 
 

time: 346 us -> 360 us (1.040)
  waiting for transfers between devices: 84.4 us -> 95.5 us
    psum x1, waiting for transfers between devices: 0.02 us -> 61.3 us  [return_plate(): summed = lax.psum(flat.astype(jnp.bfloat16), 'col').astype(jnp.float32)]
    psum x1 -> x0, waiting for transfers between devices: 52.6 us -> none  [return_tower(): summed = lax.psum(flat.astype(jnp.bfloat16), 'row').astype(jnp.float32)]
    all_gather x1, waiting for transfers between devices: 0.02 us -> 32.8 us  [shards(): lax.all_gather(features, 'col', axis=0, tiled=True).reshape(-1, CLUSTER, D)]
    all_gather x1, waiting for transfers between devices: 30.4 us -> 0.02 us  [shards(): lax.all_gather(features, 'row', axis=0, tiled=True).reshape(-1, CLUSTER, D)]
  transfers between devices with their start and end apart: 4 -> 4, of which waited for: 2 -> 2; matrix products, arithmetic and copies ran while one was open for 70% -> 68% of each run, Pallas kernels for 0% -> 0%
where the time goes in v1:
time: 360 us; the launch traced here: 356 us
  local copies, waits for them, and re-layouts  102 us (28%)
  waiting for transfers between devices  95.5 us (27%)
  other arithmetic  76.8 us (21%)
  matrix products  67 us (19%)
  between operations  13.3 us (4%)
    psum x1, waiting for transfers between devices, return_plate(): summed = lax.psum(flat.astype(jnp.bfloat16), 'col').astype(jnp.float32)  61.3 us
    scatter-add x16, other arithmetic, plate_step(): plate_acc.at[plate_at].add(plate_side(basis, tower, tower_at, plate_weight))  44.2 us
    gather x16, local copies, waits for them, and re-layouts, tower_side(): plate[plate_at]  35.1 us
    dynamic_slice x32, local copies, waits for them, and re-layouts, block_basis(): block = lax.dynamic_slice_in_dim(bins, start, group, 0)  34.4 us
    all_gather x1, waiting for transfers between devices, shards(): lax.all_gather(features, 'col', axis=0, tiled=True).reshape(-1, CLUSTER, D)  32.8 us
    gather x16, local copies, waits for them, and re-layouts, plate_side(): tower[tower_at]  29.2 us
    dot_general x16, matrix products, plate_side(): jnp.einsum('gakb,gbd->gakd', basis, tower[tower_at], preferred_element_ty...  20.9 us
    dot_general x16, matrix products, tower_side(): jnp.einsum('gakb,gad->gbkd', basis, plate[plate_at], preferred_element_ty...  20.8 us
  transfers between devices with their start and end apart: 4, of which 2 were waited for; matrix products, arithmetic and copies ran while one was open for 68% of the time, Pallas kernels for 0%

profile of v1, /device:TPU:0, one launch (start us, length us, event | category | flops | bytes accessed | tf_op | source)
XLA Modules:
  0.0 355.9 jit_solution(17244666833676168626)
XLA Ops:
  8.1 32.8 %all-gather.6.cloned.1.call-done = bf16[8192,128]{1,0:T(8,128)(2,1)} async-done(((bf16[1024,128]{1,0:T(8,128)(2,1)}), bf16[8192,128]{1,0:T(8,128)(2,1)}) %all-gather.6.cloned.1.call-update) | async-done | bytes 2097168 | tf_op jit(solution)/shard_map/all_gather | solution.py:66
  41.1 105.4 %while.27 = (s32[]{:T(128)}, f32[32,128,128]{2,1,0:T(8,128)S(1)}, s32[2,128]{1,0:T(2,128)S(1)}, bf16[64,128,128]{2,1,0:T(8,128)(2,1)}, s32[128,128,128]{2,1,0:T(...) while((s32[]{:T(128)}, f32[32,128,128]{2,1,0:T(8,128)S(1)}, ...), condition=%wide.region_6.0_spmd, body=%wide.region_4.0_spmd.sunk | while | flops 540148736 | bytes 8919471 | solution.py:82
  47.8 2.3 gather_fusion.1
  147.8 2.5 broadcast_in_dim.38
  150.3 126.6 %while.26 = (s32[]{:T(128)}, f32[64,128,128]{2,1,0:T(8,128)}, s32[2,128]{1,0:T(2,128)S(1)}, s32[128,128,128]{2,1,0:T(8,128)}, bf16[32,128,128]{2,1,0:T(8,128)(2,...) while((s32[]{:T(128)}, f32[64,128,128]{2,1,0:T(8,128)}, ...), condition=%wide.region_2.0_spmd, body=%wide.region_0.0_spmd.sunk | while | flops 540148736 | bytes 8919471 | solution.py:84
  155.4 2.9 scatter_fusion
  163.4 2.7 scatter_fusion
  171.3 2.6 scatter_fusion
  179.1 2.8 scatter_fusion
  187.0 2.8 scatter_fusion
  194.9 2.8 scatter_fusion
  202.8 2.8 scatter_fusion
  210.8 2.8 scatter_fusion
  218.7 2.8 scatter_fusion
  226.6 2.8 scatter_fusion
  234.5 2.8 scatter_fusion
  242.5 2.8 scatter_fusion
  250.4 2.8 scatter_fusion
  258.3 2.8 scatter_fusion
  266.2 2.8 scatter_fusion
  274.1 2.8 scatter_fusion
  276.9 3.9 %convert_element_type.63 = bf16[64,128,128]{2,1,0:T(8,128)(2,1)} convert(f32[64,128,128]{2,1,0:T(8,128)} %get-tuple-element.223) | non-fusion elementwise | flops 1048576 | bytes 6291456 | tf_op jit(solution)/shard_map/convert_element_type | solution.py:58
  280.9 3.5 reduce_sum.21
  284.4 61.3 %all-reduce.2.cloned.1.call-done = bf16[8192,128]{1,0:T(8,128)(2,1)} async-done(((bf16[8192,128]{1,0:T(8,128)(2,1)}), bf16[8192,128]{1,0:T(8,128)(2,1)}) %all-reduce.2.cloned.1.call-update) | async-done | bytes 2097168 | tf_op jit(solution)/shard_map/psum | solution.py:58
  (301 shorter events, 190.7 us)
Async XLA Ops:
  6.5 341.5 %copy-start = (bf16[256,128]{1,0:T(8,128)(2,1)S(1)}, bf16[256,128]{1,0:T(8,128)(2,1)}, u32[]{:S(2)}) copy-start(bf16[256,128]{1,0:T(8,128)(2,1)} %param.18) | copy-start | bytes 196612
  6.5 34.5 %copy-start.4 = (s32[2,128]{1,0:T(2,128)S(1)}, s32[2,128]{1,0:T(2,128)}, u32[]{:S(2)}) copy-start(s32[2,128]{1,0:T(2,128)} %param.13) | copy-start | bytes 3076
  6.5 34.6 %copy-start.1 = (bf16[1024,128]{1,0:T(8,128)(2,1)S(1)}, bf16[1024,128]{1,0:T(8,128)(2,1)}, u32[]{:S(2)}) copy-start(bf16[1024,128]{1,0:T(8,128)(2,1)} %param.16) | copy-start | bytes 786436
  6.5 34.3 %all-gather.6.cloned.1.call-start = ((), (), s32[]{:S(2)}) async-start(), calls=%async_computation.2 | async-start | bytes 2359296 | tf_op jit(solution)/shard_map/all_gather | solution.py:66
  7.3 140.5 %all-gather.4.cloned.1.call-start = ((), (), s32[]{:S(2)}) async-start(), calls=%async_computation | async-start | bytes 1310720 | tf_op jit(solution)/shard_map/all_gather | solution.py:67
  8.0 272.9 %all-gather.8.cloned.1.call-start = ((), (), s32[]{:S(2)}) async-start(), calls=%async_computation.3 | async-start | bytes 5242880 | tf_op jit(solution)/shard_map/all_gather | solution.py:52
  147.7 198.0 %all-reduce.2.cloned.1.call-start = ((), (), s32[]{:S(2)}) async-start(), calls=%async_computation.1 | async-start | bytes 4194304 | tf_op jit(solution)/shard_map/psum | solution.py:58
  147.8 2.5 copy-start.2
  280.9 66.0 %copy-start.5 = (f32[128]{0:T(128)S(1)}, f32[128]{0:T(128)}, u32[]{:S(2)}) copy-start(f32[128]{0:T(128)} %param.17) | copy-start | bytes 1540
  280.9 67.2 %copy-start.3 = (bf16[1024,128]{1,0:T(8,128)(2,1)S(1)}, bf16[1024,128]{1,0:T(8,128)(2,1)}, u32[]{:S(2)}) copy-start(bf16[1024,128]{1,0:T(8,128)(2,1)} %param.12) | copy-start | bytes 786436
  280.9 67.2 %copy-start.6 = (bf16[128,128]{1,0:T(8,128)(2,1)S(1)}, bf16[128,128]{1,0:T(8,128)(2,1)}, u32[]{:S(2)}) copy-start(bf16[128,128]{1,0:T(8,128)(2,1)} %param.19) | copy-start | bytes 98308
Sparse Core Ops, SparseCore 0:
  8.9 31.8 all-gather.5
  42.7 25.8 all-gather.3
  147.8 52.0 all-gather.7
  281.0 64.6 all-reduce.1
